TPU v7x, 32 devices: a whole 2x2x4 slice. The times are simulated.
32 devices in a mesh: expert: 8 (over z, x), hidden: 4 (over y, core).
Axes of the slice: x: 2, y: 2, z: 4, core: 2. Of those that a mesh axis runs over, the one named last changes fastest.
Arguments:
- tokens: bfloat16 [768, 4096], P('expert', 'hidden'), may hold values from -6 to 6
- gate_weight: bfloat16 [16, 4096, 1536], P('expert', None, 'hidden'), may hold values from -0.09375 to 0.09375
- up_weight: bfloat16 [16, 4096, 1536], P('expert', None, 'hidden'), may hold values from -0.09375 to 0.09375
- down_weight: bfloat16 [16, 1536, 4096], P('expert', 'hidden'), may hold values from -0.15625 to 0.15625
- swap_slot: int32 [8], replicated, may hold values from 0 to 1
- expert_ids: int32 [768, 8], P('expert'), may hold values from 0 to 15, as said below
- gate_fixed: int32 [768, 8], P('expert'), may hold values from 1 to 65535
Outputs:
- moe_out: bfloat16 [768, 4096], P('expert', 'hidden')
Inputs may be any that keep to these rules, and one draw needn't show every extreme that they name: `expert_ids`: each row names 8 ids on 8 different indices of the expert axis (index = id // 2). In the 96 rows of each index of the expert axis, every index is named exactly 96 times.
All inputs are finite; a program needn't handle non-finite values.
Results may differ from a plain program's by a relative error of at most 0.012.
Values may be sent and summed in bfloat16 or wider, within the bound.
A program may use at most 192 MiB of HBM per device.

v0:
```python
import jax
import jax.numpy as jnp
from jax import lax
from jax.sharding import PartitionSpec as P


def slot_weights(expert_ids, gate_fixed, swap_slot, slots_here):
    axis_count = lax.axis_size("expert")
    me = lax.axis_index("expert")
    scores = gate_fixed.astype(jnp.float32)
    gate_norm = scores / jnp.sum(scores, axis=1, keepdims=True)
    home = expert_ids // slots_here
    slot = expert_ids % slots_here
    onehot = home[:, :, None] == jnp.arange(axis_count, dtype=jnp.int32)
    own_swap = jnp.sum(jnp.where(onehot, swap_slot, 0), axis=2)
    other_swap = jnp.sum(jnp.where(onehot, jnp.roll(swap_slot, -(axis_count // 2)), 0), axis=2)
    other = (home + axis_count // 2) % axis_count
    source = jnp.where(slot == own_swap, other * slots_here + other_swap, expert_ids)
    mine = me * slots_here + jnp.arange(slots_here, dtype=jnp.int32)
    return jnp.sum(jnp.where(source[:, :, None] == mine, gate_norm[:, :, None], 0.0), axis=1)


def per_device(tokens, gate_weight, up_weight, down_weight, swap_slot, expert_ids, gate_fixed):
    slots_here = gate_weight.shape[0]
    ids_all = lax.all_gather(expert_ids, "expert", axis=0, tiled=True)
    gates_all = lax.all_gather(gate_fixed, "expert", axis=0, tiled=True)
    weight = slot_weights(ids_all, gates_all, swap_slot, slots_here)
    rows = lax.all_gather(tokens, "hidden", axis=1, tiled=True)
    rows = lax.all_gather(rows, "expert", axis=0, tiled=True)
    total = None
    for s in range(slots_here):
        gate_out = jnp.dot(rows, gate_weight[s], preferred_element_type=jnp.float32)
        up_out = jnp.dot(rows, up_weight[s], preferred_element_type=jnp.float32)
        hidden = (jax.nn.silu(gate_out) * up_out * weight[:, s : s + 1]).astype(jnp.bfloat16)
        out = jnp.dot(hidden, down_weight[s], preferred_element_type=jnp.float32)
        total = out if total is None else total + out
    total = total.astype(jnp.bfloat16)
    part = lax.psum_scatter(total, "expert", scatter_dimension=0, tiled=True)
    return lax.psum_scatter(part, "hidden", scatter_dimension=1, tiled=True)


def solution(mesh):
    in_specs = (
        P("expert", "hidden"),
        P("expert", None, "hidden"),
        P("expert", None, "hidden"),
        P("expert", "hidden", None),
        P(),
        P("expert", None),
        P("expert", None),
    )
    return jax.shard_map(
        per_device, mesh=mesh, in_specs=in_specs, out_specs=P("expert", "hidden"), check_vma=False
    )
```

profile of v0, /device:TPU:0, one launch (start us, length us, event | category | flops | bytes accessed | tf_op | source)
XLA Modules:
  0.0 301.3 jit_solution(4140914008804489191)
XLA Ops:
  6.5 0.0 all-gather.4.cloned.1.call-start
  6.5 11.7 %all_gather.12 = bf16[96,4096]{1,0:T(8,128)(2,1)} all-gather(bf16[96,1024]{1,0:T(8,128)(2,1)} %param.7), channel_id=1, replica_groups=mesh['expert'=8,'hidden'=4] {'hidden'}, dimensions={1}, use_global_device_ids=true | all-gather | bytes 983040 | tf_op jit(solution)/shard_map/all_gather | solution.py:28
  18.2 0.0 all-gather.4.cloned.1.call-update
  18.3 0.0 reduce-scatter.3.cloned.1.call-start
  18.3 31.5 %all-gather.1 = s32[8,96,8]{1,2,0:T(8,128)S(1)} all-gather(s32[1,96,8]{1,2,0:T(8,128)} %bitcast.44), channel_id=1, replica_groups=mesh['expert'=8,'hidden'=4] {'expert'}, dimensions={0}, use_global_device_ids=true | all-gather | bytes 27648 | tf_op jit(solution)/shard_map/all_gather | solution.py:26
  49.8 0.1 reshape.12
  49.9 0.1 reshape.13
  50.0 30.9 %all-gather = s32[8,96,8]{1,2,0:T(8,128)S(1)} all-gather(s32[1,96,8]{1,2,0:T(8,128)} %bitcast.45), channel_id=1, replica_groups=mesh['expert'=8,'hidden'=4] {'expert'}, dimensions={0}, use_global_device_ids=true | all-gather | bytes 27648 | tf_op jit(solution)/shard_map/all_gather | solution.py:25
  80.9 0.1 reshape.9
  81.0 0.8 fusion.42
  81.8 0.1 pad_add_fusion
  81.9 0.8 select_reduce_fusion.1
  82.8 0.1 select_reduce_fusion.2
  82.9 35.3 %all-gather.4.cloned.1.call-done = bf16[768,4096]{1,0:T(8,128)(2,1)} async-done(((bf16[96,4096]{1,0:T(8,128)(2,1)}), bf16[768,4096]{1,0:T(8,128)(2,1)}) %all-gather.4.cloned.1.call-update) | async-done | bytes 6291472 | tf_op jit(solution)/shard_map/all_gather | solution.py:29
  118.2 0.0 copy-start
  118.2 0.0 slice-start
  118.2 0.0 slice-start.2
  118.2 6.6 %fusion.9 = f32[768,384]{1,0:T(8,128)S(1)} fusion(bf16[768,4096]{1,0:T(8,128)(2,1)} %all-gather.4.cloned.1.call-done, bf16[2,4096,384]{2,1,0:T(8,128)(2,1)} %param.8), kind=kOutput, calls=%fused_computation.10 | convolution fusion | flops 2415919104 | bytes 10616832 | tf_op jit(solution)/shard_map/dot_general | solution.py:32
  124.8 0.0 copy-done
  124.8 0.0 slice-start.1
  124.8 0.0 slice-start.3
  124.8 5.8 %fusion.29 = bf16[768,384]{1,0:T(8,128)(2,1)S(1)} fusion(bf16[768,4096]{1,0:T(8,128)(2,1)S(1)} %copy-done, bf16[2,4096,384]{2,1,0:T(8,128)(2,1)} %param.9, f32[768,384]{1,0:T(8,128)S(1)} %fusion.9, f32[768]{0:T(1024)S(1)} %get-tuple-element.8), kind=kOutput, calls=%fused_computation.22 | convolution fusion | flops 2417983488 | bytes 11209728 | tf_op jit(solution)/shard_map/dot_general | solution.py:33
  130.6 0.0 slice-done
  130.6 0.0 slice-done.1
  130.7 0.0 slice-start.4
  130.7 3.4 %fusion.5 = f32[768,4096]{1,0:T(8,128)S(1)} fusion(bf16[768,384]{1,0:T(8,128)(2,1)S(1)} %fusion.29, bf16[2,384,4096]{2,1,0:T(8,128)(2,1)S(1)} %bitcast.43), kind=kOutput, calls=%fused_computation.6 | convolution fusion | flops 2415919104 | bytes 16318464 | tf_op jit(solution)/shard_map/dot_general | solution.py:35
  134.1 0.0 slice-done.2
  134.1 0.0 slice-done.3
  134.1 0.0 slice-start.5
  134.2 5.7 %fusion.3 = f32[768,384]{1,0:T(8,128)S(1)} fusion(bf16[768,4096]{1,0:T(8,128)(2,1)} %all-gather.4.cloned.1.call-done, bf16[2,4096,384]{2,1,0:T(8,128)(2,1)S(1)} %bitcast.47), kind=kOutput, calls=%fused_computation.4 | convolution fusion | flops 2415919104 | bytes 10616832 | tf_op jit(solution)/shard_map/dot_general | solution.py:32
  139.8 0.0 slice-done.4
  139.9 0.0 slice-done.5
  139.9 6.3 %fusion.32 = bf16[768,384]{1,0:T(8,128)(2,1)S(1)} fusion(bf16[768,4096]{1,0:T(8,128)(2,1)} %all-gather.4.cloned.1.call-done, bf16[2,4096,384]{2,1,0:T(8,128)(2,1)S(1)} %bitcast.49, f32[768,384]{1,0:T(8,128)S(1)} %fusion.3, f32[768]{0:T(1024)S(1)} %get-tuple-element.7), kind=kOutput, calls=%fused_computation.23 | convolution fusion | flops 2417983488 | bytes 11210752 | tf_op jit(solution)/shard_map/dot_general | solution.py:33
  146.2 7.3 %add_convert_fusion = bf16[768,4096]{1,0:T(8,128)(2,1)} fusion(f32[768,4096]{1,0:T(8,128)S(1)} %fusion.5, bf16[768,384]{1,0:T(8,128)(2,1)S(1)} %fusion.32, bf16[2,384,4096]{2,1,0:T(8,128)(2,1)} %param.10), kind=kOutput, calls=%fused_computation | convolution fusion | flops 2422210560 | bytes 22609920 | tf_op jit(solution)/shard_map/dot_general | solution.py:35
  153.5 0.0 reduce-scatter.3.cloned.1.call-update
  153.5 0.0 reduce-scatter.5.cloned.1.call-start
  153.6 116.3 %reduce-scatter.3.cloned.1.call-done = bf16[96,4096]{1,0:T(8,128)(2,1)} async-done(((bf16[768,4096]{1,0:T(8,128)(2,1)}), bf16[96,4096]{1,0:T(8,128)(2,1)}) %reduce-scatter.3.cloned.1.call-update) | async-done | bytes 786448 | tf_op jit(solution)/shard_map/reduce_scatter | solution.py:38
  269.9 0.0 reduce-scatter.5.cloned.1.call-update
  269.9 24.9 %reduce-scatter.5.cloned.1.call-done = bf16[96,1024]{1,0:T(8,128)(2,1)} async-done(((bf16[96,4096]{1,0:T(8,128)(2,1)}), bf16[96,1024]{1,0:T(8,128)(2,1)}) %reduce-scatter.5.cloned.1.call-update) | async-done | bytes 196624 | tf_op jit(solution)/shard_map/reduce_scatter | solution.py:39
  (12 shorter events, 0.1 us)
Async XLA Ops:
  6.5 111.7 %all-gather.4.cloned.1.call-start = ((), (), s32[]{:S(2)}) async-start(), calls=%async_computation.2 | async-start | bytes 7077888 | tf_op jit(solution)/shard_map/all_gather | solution.py:29
  18.3 251.6 %reduce-scatter.3.cloned.1.call-start = ((), (), s32[]{:S(2)}) async-start(), calls=%async_computation.3 | async-start | bytes 7077888 | tf_op jit(solution)/shard_map/reduce_scatter | solution.py:38
  118.2 6.6 %copy-start = (bf16[768,4096]{1,0:T(8,128)(2,1)S(1)}, bf16[768,4096]{1,0:T(8,128)(2,1)}, u32[]{:S(2)}) copy-start(bf16[768,4096]{1,0:T(8,128)(2,1)} %all-gather.4.cloned.1.call-done) | copy-start | bytes 18874372
  118.2 12.4 %slice-start = ((s8[6291456]{0:T(1024)(128)(4,1)}), s8[4194304]{0:T(1024)(128)(4,1)S(1)}, s32[]{:S(2)}) async-start(s8[6291456]{0:T(1024)(128)(4,1)} %bitcast.42), calls=%async_computation.5 | async-start | bytes 8388608
  118.2 15.9 %slice-start.2 = ((s8[6291456]{0:T(1024)(128)(4,1)}), s8[4194304]{0:T(1024)(128)(4,1)S(1)}, s32[]{:S(2)}) async-start(s8[6291456]{0:T(1024)(128)(4,1)} %bitcast.46), calls=%async_computation.7 | async-start | bytes 8388608
  124.8 5.8 %slice-start.1 = ((s8[6291456]{0:T(1024)(128)(4,1)}), s8[2097152]{0:T(1024)(128)(4,1)S(1)}, s32[]{:S(2)}) async-start(s8[6291456]{0:T(1024)(128)(4,1)} %bitcast.42), calls=%async_computation.6 | async-start | bytes 4194304
  124.8 9.3 %slice-start.3 = ((s8[6291456]{0:T(1024)(128)(4,1)}), s8[2097152]{0:T(1024)(128)(4,1)S(1)}, s32[]{:S(2)}) async-start(s8[6291456]{0:T(1024)(128)(4,1)} %bitcast.46), calls=%async_computation.8 | async-start | bytes 4194304
  130.7 9.2 %slice-start.4 = ((s8[6291456]{0:T(1024)(128)(4,1)}), s8[2097152]{0:T(1024)(128)(4,1)S(1)}, s32[]{:S(2)}) async-start(s8[6291456]{0:T(1024)(128)(4,1)} %bitcast.48), calls=%async_computation.9 | async-start | bytes 4194304
  134.1 5.7 %slice-start.5 = ((s8[6291456]{0:T(1024)(128)(4,1)}), s8[4194304]{0:T(1024)(128)(4,1)S(1)}, s32[]{:S(2)}) async-start(s8[6291456]{0:T(1024)(128)(4,1)} %bitcast.48), calls=%async_computation.10 | async-start | bytes 8388608
  153.5 141.3 %reduce-scatter.5.cloned.1.call-start = ((), (), s32[]{:S(2)}) async-start(), calls=%async_computation.4 | async-start | bytes 983040 | tf_op jit(solution)/shard_map/reduce_scatter | solution.py:39
Sparse Core Ops, SparseCore 0:
  18.4 99.7 all-gather.3
  153.6 116.1 reduce-scatter.2
  272.4 22.3 reduce-scatter.4
where the time goes:
time: 302 us; the launch traced here: 301 us
  waiting for transfers between devices  177 us (59%)
  blocking collectives  74.1 us (25%)
  matrix products  35.1 us (12%)
  between operations  13.3 us (4%)
    reduce_scatter x1, waiting for transfers between devices, per_device(): part = lax.psum_scatter(total, 'expert', scatter_dimension=0, tiled=True)  116 us
    all_gather x1, waiting for transfers between devices, per_device(): rows = lax.all_gather(rows, 'expert', axis=0, tiled=True)  35.3 us
    all_gather x1, blocking collectives, per_device(): gates_all = lax.all_gather(gate_fixed, 'expert', axis=0, tiled=True)  31.5 us
    all_gather x1, blocking collectives, per_device(): ids_all = lax.all_gather(expert_ids, 'expert', axis=0, tiled=True)  30.9 us
    reduce_scatter x1, waiting for transfers between devices, per_device(): return lax.psum_scatter(part, 'hidden', scatter_dimension=1, tiled=True)  24.9 us
    dot_general x2, matrix products, per_device(): gate_out = jnp.dot(rows, gate_weight[s], preferred_element_type=jnp.float32)  12.2 us
    dot_general x2, matrix products, per_device(): up_out = jnp.dot(rows, up_weight[s], preferred_element_type=jnp.float32)  12.1 us
    all_gather x1, blocking collectives, per_device(): rows = lax.all_gather(tokens, 'hidden', axis=1, tiled=True)  11.7 us
  transfers between devices with their start and end apart: 3, of which 3 were waited for; matrix products, arithmetic and copies ran while one was open for 1% of the time, Pallas kernels for 0%

commit v1 on v0

--- a/solution.py
+++ b/solution.py
@@ -2,6 +2,27 @@
 import jax.numpy as jnp
 from jax import lax
 from jax.sharding import PartitionSpec as P
+
+
+def ring_gather(x, axis, dim):
+    devices, index, span = (lax.axis_size(axis), lax.axis_index(axis), x.shape[dim])
+    upward = [(i, (i + 1) % devices) for i in range(devices)]
+    behind = [(i, (i - 1) % devices) for i in range(devices)]
+    out = jnp.zeros((*x.shape[:dim], devices * span, *x.shape[dim + 1 :]), x.dtype)
+    out = lax.dynamic_update_slice_in_dim(out, x, index * span, axis=dim)
+    from_left = from_right = x
+    half = devices // 2
+    for hop in range(1, half + 1):
+        from_left = lax.ppermute(from_left, axis, upward)
+        out = lax.dynamic_update_slice_in_dim(
+            out, from_left, (index - hop) % devices * span, axis=dim
+        )
+        if hop < devices - half:
+            from_right = lax.ppermute(from_right, axis, behind)
+            out = lax.dynamic_update_slice_in_dim(
+                out, from_right, (index + hop) % devices * span, axis=dim
+            )
+    return out
 
 
 def slot_weights(expert_ids, gate_fixed, swap_slot, slots_here):
@@ -26,7 +47,7 @@
     gates_all = lax.all_gather(gate_fixed, "expert", axis=0, tiled=True)
     weight = slot_weights(ids_all, gates_all, swap_slot, slots_here)
     rows = lax.all_gather(tokens, "hidden", axis=1, tiled=True)
-    rows = lax.all_gather(rows, "expert", axis=0, tiled=True)
+    rows = ring_gather(rows, "expert", 0)
     total = None
     for s in range(slots_here):
         gate_out = jnp.dot(rows, gate_weight[s], preferred_element_type=jnp.float32)

time: 302 us -> 367 us (1.22)
  starting transfers between devices: 0.09 us -> 27.6 us
  waiting for transfers between devices: 177 us -> 200 us
  blocking collectives: 74.1 us -> 97 us
  matrix products: 35.1 us -> 24.8 us
    ppermute x0 -> x7, waiting for transfers between devices: none -> 58.4 us  [the longest x4 38.7 us: ring_gather(): from_left = lax.ppermute(from_left, axis, upward)]
    all_gather x1 -> x0, waiting for transfers between devices: 35.3 us -> none  [per_device(): rows = lax.all_gather(rows, 'expert', axis=0, tiled=True)]
    ppermute x0 -> x7, starting transfers between devices: none -> 27.6 us  [the longest x3 25.1 us: ring_gather(): from_right = lax.ppermute(from_right, axis, behind)]
    all_gather x1, blocking collectives: 31.5 us -> 56.1 us  [per_device(): gates_all = lax.all_gather(gate_fixed, 'expert', axis=0, tiled=True)]
    dot_general x2, matrix products: 12.2 us -> 6.85 us  [per_device(): gate_out = jnp.dot(rows, gate_weight[s], preferred_element_type=jnp.float32)]
    dot_general x2, matrix products: 12.1 us -> 6.85 us  [per_device(): up_out = jnp.dot(rows, up_weight[s], preferred_element_type=jnp.float32)]
  transfers between devices with their start and end apart: 3 -> 9, of which waited for: 3 -> 5; matrix products, arithmetic and copies ran while one was open for 1% -> 1% of each run, Pallas kernels for 0% -> 0%
where the time goes in v1:
time: 367 us
  waiting for transfers between devices  200 us (54%)
  blocking collectives  97 us (26%)
  starting transfers between devices  27.6 us (8%)
  matrix products  24.8 us (7%)
  between operations  13.7 us (4%)
    reduce_scatter x1, waiting for transfers between devices, per_device(): part = lax.psum_scatter(total, 'expert', scatter_dimension=0, tiled=True)  117 us
    all_gather x1, blocking collectives, per_device(): gates_all = lax.all_gather(gate_fixed, 'expert', axis=0, tiled=True)  56.1 us
    ppermute x4, waiting for transfers between devices, ring_gather(): from_left = lax.ppermute(from_left, axis, upward)  38.7 us
    all_gather x1, blocking collectives, per_device(): ids_all = lax.all_gather(expert_ids, 'expert', axis=0, tiled=True)  30.6 us
    ppermute x3, starting transfers between devices, ring_gather(): from_right = lax.ppermute(from_right, axis, behind)  25.1 us
    reduce_scatter x1, waiting for transfers between devices, per_device(): return lax.psum_scatter(part, 'hidden', scatter_dimension=1, tiled=True)  24.9 us
    ppermute x3, waiting for transfers between devices, ring_gather(): from_right = lax.ppermute(from_right, axis, behind)  19.7 us
    dot_general x2, matrix products, per_device(): out = jnp.dot(hidden, down_weight[s], preferred_element_type=jnp.float32)  11.1 us
  transfers between devices with their start and end apart: 9, of which 5 were waited for; matrix products, arithmetic and copies ran while one was open for 1% of the time, Pallas kernels for 0%

profile of v1, /device:TPU:0, one launch (start us, length us, event | category | flops | bytes accessed | tf_op | source)
XLA Modules:
  0.0 367.0 jit_solution(16371602885482716476)
XLA Ops:
  6.5 0.0 reduce-scatter.3.cloned.1.call-start
  6.5 10.3 %all_gather.9 = bf16[96,4096]{1,0:T(8,128)(2,1)S(1)} all-gather(bf16[96,1024]{1,0:T(8,128)(2,1)} %param.7), channel_id=1, replica_groups=mesh['expert'=8,'hidden'=4] {'hidden'}, dimensions={1}, use_global_device_ids=true | all-gather | bytes 983040 | tf_op jit(solution)/shard_map/all_gather | solution.py:49
  16.8 4.5 %collective-permute-start.1 = (bf16[96,4096]{1,0:T(8,128)(2,1)S(1)}, bf16[96,4096]{1,0:T(8,128)(2,1)S(1)}, u32[]{:S(2)}, u32[]{:S(2)}) collective-permute-start(bf16[96,4096]{1,0:T(8,128)(2,1)S(1)} %all_gather.9), channel_id=1, source_target_pairs={{0,28},{4,0},{8,4},{12,8},{16,12},{20,16},{24,20},{28,24},{1,29},{... | collective-permute-start | bytes 2359304 | tf_op jit(solution)/shard_map/ppermute | solution.py:21
  21.3 0.0 collective-permute-start
  21.3 56.1 %all-gather.1 = s32[8,96,8]{1,2,0:T(8,128)S(1)} all-gather(s32[1,96,8]{1,2,0:T(8,128)} %bitcast.30), channel_id=1, replica_groups=mesh['expert'=8,'hidden'=4] {'expert'}, dimensions={0}, use_global_device_ids=true | all-gather | bytes 27648 | tf_op jit(solution)/shard_map/all_gather | solution.py:47
  77.5 0.8 fusion.30
  78.3 0.1 reshape.12
  78.4 0.1 reshape.13
  78.5 30.6 %all-gather = s32[8,96,8]{1,2,0:T(8,128)S(1)} all-gather(s32[1,96,8]{1,2,0:T(8,128)} %bitcast.31), channel_id=1, replica_groups=mesh['expert'=8,'hidden'=4] {'expert'}, dimensions={0}, use_global_device_ids=true | all-gather | bytes 27648 | tf_op jit(solution)/shard_map/all_gather | solution.py:46
  109.1 0.1 reshape.9
  109.2 0.1 pad_add_fusion
  109.3 0.8 select_reduce_fusion.1
  110.2 0.1 select_reduce_fusion.2
  110.4 0.0 slice-start.2
  110.4 0.8 broadcast_in_dim.33
  111.1 0.1 constant_dynamic-update-slice_fusion.7
  111.2 0.0 collective-permute-done.1
  111.2 8.2 %collective-permute-start.3 = (bf16[96,4096]{1,0:T(8,128)(2,1)S(1)}, bf16[96,4096]{1,0:T(8,128)(2,1)S(1)}, u32[]{:S(2)}, u32[]{:S(2)}) collective-permute-start(bf16[96,4096]{1,0:T(8,128)(2,1)S(1)} %collective-permute-done.1), channel_id=1, source_target_pairs={{0,28},{4,0},{8,4},{12,8},{16,12},{20,16},{24,20},{28,24},{1,29},{... | collective-permute-start | bytes 2359304 | tf_op jit(solution)/shard_map/ppermute | solution.py:21
  119.4 0.0 collective-permute-done
  119.4 0.0 collective-permute-start.2
  119.4 0.1 constant_dynamic-update-slice_fusion.6
  119.5 0.0 slice-start.3
  119.5 0.1 constant_dynamic-update-slice_fusion.5
  119.6 19.7 %collective-permute-done.3 = bf16[96,4096]{1,0:T(8,128)(2,1)S(1)} collective-permute-done((bf16[96,4096]{1,0:T(8,128)(2,1)S(1)}, bf16[96,4096]{1,0:T(8,128)(2,1)S(1)}, u32[]{:S(2)}, u32[]{:S(2)}) %collective-permute-start.3) | collective-permute-done | bytes 786464 | tf_op jit(solution)/shard_map/ppermute | solution.py:21
  139.3 12.4 %collective-permute-start.5 = (bf16[96,4096]{1,0:T(8,128)(2,1)S(1)}, bf16[96,4096]{1,0:T(8,128)(2,1)S(1)}, u32[]{:S(2)}, u32[]{:S(2)}) collective-permute-start(bf16[96,4096]{1,0:T(8,128)(2,1)S(1)} %collective-permute-done.3), channel_id=1, source_target_pairs={{0,28},{4,0},{8,4},{12,8},{16,12},{20,16},{24,20},{28,24},{1,29},{... | collective-permute-start | bytes 2359304 | tf_op jit(solution)/shard_map/ppermute | solution.py:21
  151.8 0.0 collective-permute-done.2
  151.8 0.0 collective-permute-start.4
  151.8 0.1 constant_dynamic-update-slice_fusion.4
  151.8 0.1 constant_dynamic-update-slice_fusion.3
  151.9 25.5 %collective-permute-done.4 = bf16[96,4096]{1,0:T(8,128)(2,1)S(1)} collective-permute-done((bf16[96,4096]{1,0:T(8,128)(2,1)S(1)}, bf16[96,4096]{1,0:T(8,128)(2,1)S(1)}, u32[]{:S(2)}, u32[]{:S(2)}) %collective-permute-start.4) | collective-permute-done | bytes 786464 | tf_op jit(solution)/shard_map/ppermute | solution.py:16
  177.4 2.5 collective-permute-start.6
  179.9 0.1 constant_dynamic-update-slice_fusion.2
  179.9 0.0 collective-permute-done.5
  179.9 0.1 constant_dynamic-update-slice_fusion.1
  180.0 13.2 %collective-permute-done.6 = bf16[96,4096]{1,0:T(8,128)(2,1)S(1)} collective-permute-done((bf16[96,4096]{1,0:T(8,128)(2,1)S(1)}, bf16[96,4096]{1,0:T(8,128)(2,1)S(1)}, u32[]{:S(2)}, u32[]{:S(2)}) %collective-permute-start.6) | collective-permute-done | bytes 786464 | tf_op jit(solution)/shard_map/ppermute | solution.py:16
  193.2 0.1 constant_dynamic-update-slice_fusion
  193.3 0.0 slice-done.2
  193.3 0.0 slice-done.3
  193.3 0.0 slice-start.4
  193.3 3.4 fusion.1
  196.8 0.0 slice-start.5
  196.8 3.4 fusion.7
  200.2 0.0 slice-done.4
  200.2 0.0 slice-done.5
  200.2 0.0 slice-start
  200.2 3.4 fusion.3
  203.7 0.0 slice-start.1
  203.7 3.4 fusion.9
  207.1 0.0 slice-done
  207.1 0.0 slice-done.1
  207.1 3.5 fusion.5
  210.7 7.6 %add_convert_fusion = bf16[768,4096]{1,0:T(8,128)(2,1)} fusion(f32[768,4096]{1,0:T(8,128)S(1)} %fusion.5, bf16[2,384,4096]{2,1,0:T(8,128)(2,1)} %param.10, f32[768,384]{1,0:T(8,128)S(1)} %fusion.1, f32[768,384]{1,0:T(8,128)S(1)} %fusion.3, f32[768]{0:T(1024)S(1)} %get-tuple-element.7), kind=kOutput, calls=%fused_computation | convolution fusion | flops 2424274944 | bytes 24382464 | tf_op jit(solution)/shard_map/dot_general | solution.py:56
  218.3 0.0 reduce-scatter.3.cloned.1.call-update
  218.3 0.0 reduce-scatter.5.cloned.1.call-start
  218.4 116.9 %reduce-scatter.3.cloned.1.call-done = bf16[96,4096]{1,0:T(8,128)(2,1)} async-done(((bf16[768,4096]{1,0:T(8,128)(2,1)}), bf16[96,4096]{1,0:T(8,128)(2,1)}) %reduce-scatter.3.cloned.1.call-update) | async-done | bytes 786448 | tf_op jit(solution)/shard_map/reduce_scatter | solution.py:59
  335.2 0.0 reduce-scatter.5.cloned.1.call-update
  335.2 24.9 %reduce-scatter.5.cloned.1.call-done = bf16[96,1024]{1,0:T(8,128)(2,1)} async-done(((bf16[96,4096]{1,0:T(8,128)(2,1)}), bf16[96,1024]{1,0:T(8,128)(2,1)}) %reduce-scatter.5.cloned.1.call-update) | async-done | bytes 196624 | tf_op jit(solution)/shard_map/reduce_scatter | solution.py:60
  (12 shorter events, 0.1 us)
Async XLA Ops:
  6.5 328.7 %reduce-scatter.3.cloned.1.call-start = ((), (), s32[]{:S(2)}) async-start(), calls=%async_computation.2 | async-start | bytes 7077888 | tf_op jit(solution)/shard_map/reduce_scatter | solution.py:59
  16.8 94.4 %collective-permute-start.1 = (bf16[96,4096]{1,0:T(8,128)(2,1)S(1)}, bf16[96,4096]{1,0:T(8,128)(2,1)S(1)}, u32[]{:S(2)}, u32[]{:S(2)}) collective-permute-start(bf16[96,4096]{1,0:T(8,128)(2,1)S(1)} %all_gather.9), channel_id=1, source_target_pairs={{0,28},{4,0},{8,4},{12,8},{16,12},{20,16},{24,20},{28,24},{1,29},{... | collective-permute-start | bytes 2359304 | tf_op jit(solution)/shard_map/ppermute | solution.py:21
  21.3 98.1 %collective-permute-start = (bf16[96,4096]{1,0:T(8,128)(2,1)S(1)}, bf16[96,4096]{1,0:T(8,128)(2,1)S(1)}, u32[]{:S(2)}, u32[]{:S(2)}) collective-permute-start(bf16[96,4096]{1,0:T(8,128)(2,1)S(1)} %all_gather.9), channel_id=1, source_target_pairs={{0,4},{4,8},{8,12},{12,16},{16,20},{20,24},{24,28},{28,0},{1,5},{5... | collective-permute-start | bytes 2359304 | tf_op jit(solution)/shard_map/ppermute | solution.py:16
  110.4 82.9 %slice-start.2 = ((s8[6291456]{0:T(1024)(128)(4,1)}), s8[2097152]{0:T(1024)(128)(4,1)S(1)}, s32[]{:S(2)}) async-start(s8[6291456]{0:T(1024)(128)(4,1)} %bitcast.32), calls=%async_computation.6 | async-start | bytes 4194304
  111.2 28.1 %collective-permute-start.3 = (bf16[96,4096]{1,0:T(8,128)(2,1)S(1)}, bf16[96,4096]{1,0:T(8,128)(2,1)S(1)}, u32[]{:S(2)}, u32[]{:S(2)}) collective-permute-start(bf16[96,4096]{1,0:T(8,128)(2,1)S(1)} %collective-permute-done.1), channel_id=1, source_target_pairs={{0,28},{4,0},{8,4},{12,8},{16,12},{20,16},{24,20},{28,24},{1,29},{... | collective-permute-start | bytes 2359304 | tf_op jit(solution)/shard_map/ppermute | solution.py:21
  119.4 32.3 %collective-permute-start.2 = (bf16[96,4096]{1,0:T(8,128)(2,1)S(1)}, bf16[96,4096]{1,0:T(8,128)(2,1)S(1)}, u32[]{:S(2)}, u32[]{:S(2)}) collective-permute-start(bf16[96,4096]{1,0:T(8,128)(2,1)S(1)} %collective-permute-done), channel_id=1, source_target_pairs={{0,4},{4,8},{8,12},{12,16},{16,20},{20,24},{24,28},{28,0},{1,5},{5... | collective-permute-start | bytes 2359304 | tf_op jit(solution)/shard_map/ppermute | solution.py:16
  119.5 73.8 %slice-start.3 = ((s8[6291456]{0:T(1024)(128)(4,1)}), s8[4194304]{0:T(1024)(128)(4,1)S(1)}, s32[]{:S(2)}) async-start(s8[6291456]{0:T(1024)(128)(4,1)} %bitcast.32), calls=%async_computation.7 | async-start | bytes 8388608
  139.3 40.6 %collective-permute-start.5 = (bf16[96,4096]{1,0:T(8,128)(2,1)S(1)}, bf16[96,4096]{1,0:T(8,128)(2,1)S(1)}, u32[]{:S(2)}, u32[]{:S(2)}) collective-permute-start(bf16[96,4096]{1,0:T(8,128)(2,1)S(1)} %collective-permute-done.3), channel_id=1, source_target_pairs={{0,28},{4,0},{8,4},{12,8},{16,12},{20,16},{24,20},{28,24},{1,29},{... | collective-permute-start | bytes 2359304 | tf_op jit(solution)/shard_map/ppermute | solution.py:21
  151.8 25.6 %collective-permute-start.4 = (bf16[96,4096]{1,0:T(8,128)(2,1)S(1)}, bf16[96,4096]{1,0:T(8,128)(2,1)S(1)}, u32[]{:S(2)}, u32[]{:S(2)}) collective-permute-start(bf16[96,4096]{1,0:T(8,128)(2,1)S(1)} %collective-permute-done.2), channel_id=1, source_target_pairs={{0,4},{4,8},{8,12},{12,16},{16,20},{20,24},{24,28},{28,0},{1,5},{5... | collective-permute-start | bytes 2359304 | tf_op jit(solution)/shard_map/ppermute | solution.py:16
  177.4 15.8 %collective-permute-start.6 = (bf16[96,4096]{1,0:T(8,128)(2,1)S(1)}, bf16[96,4096]{1,0:T(8,128)(2,1)S(1)}, u32[]{:S(2)}, u32[]{:S(2)}) collective-permute-start(bf16[96,4096]{1,0:T(8,128)(2,1)S(1)} %collective-permute-done.4), channel_id=1, source_target_pairs={{0,4},{4,8},{8,12},{12,16},{16,20},{20,24},{24,28},{28,0},{1,5},{5... | collective-permute-start | bytes 2359304 | tf_op jit(solution)/shard_map/ppermute | solution.py:16
  193.3 6.9 %slice-start.4 = ((s8[6291456]{0:T(1024)(128)(4,1)}), s8[4194304]{0:T(1024)(128)(4,1)S(1)}, s32[]{:S(2)}) async-start(s8[6291456]{0:T(1024)(128)(4,1)} %bitcast.34), calls=%async_computation.8 | async-start | bytes 8388608
  196.8 3.5 slice-start.5
  200.2 6.9 %slice-start = ((s8[6291456]{0:T(1024)(128)(4,1)}), s8[4194304]{0:T(1024)(128)(4,1)S(1)}, s32[]{:S(2)}) async-start(s8[6291456]{0:T(1024)(128)(4,1)} %bitcast.28), calls=%async_computation.4 | async-start | bytes 8388608
  203.7 3.5 slice-start.1
  218.3 141.9 %reduce-scatter.5.cloned.1.call-start = ((), (), s32[]{:S(2)}) async-start(), calls=%async_computation.3 | async-start | bytes 983040 | tf_op jit(solution)/shard_map/reduce_scatter | solution.py:60
Sparse Core Ops, SparseCore 0:
  218.4 116.7 reduce-scatter.2
  337.7 22.3 reduce-scatter.4
